TPU v7x, 256 devices: a whole 4x4x8 slice. The times are simulated.
256 devices in a mesh: member: 16 (over y_lo, x, core), tile: 16 (over y_hi, z).
Axes of the slice: x: 4, y: 4 (y_hi: 2, y_lo: 2; y = y_hi * 2 + y_lo), z: 8, core: 2. Of those that a mesh axis runs over, the one named last changes fastest.
Arguments:
- atmos_state: float32 [16, 4, 128, 72, 256], P('member', None, 'tile'), may hold values from -6 to 6
- ocean_slots: float32 [16, 4, 128, 62, 256], P('member', None, 'tile'), may hold values from -6 to 6
- owner_map: int32 [16], P('tile'), may hold values from 0 to 15
- land_mask: int32 [128, 256], P('tile'), may hold values 0 or 1
- transfer_coefficient: float32 [128, 256], P('tile'), may hold values from 0.5 to 2
- air_mixing: float32 [72, 72], replicated, may hold values from -0.75 to 0.75
- sea_mixing: float32 [62, 62], replicated, may hold values from -0.75 to 0.75
Outputs:
- atmos_next: float32 [16, 4, 128, 72, 256], P('member', None, 'tile')
- ocean_next: float32 [16, 4, 128, 62, 256], P('member', None, 'tile')
Inputs may be any that keep to these rules, and one draw needn't show every extreme that they name: owner_map[t] is the member whose slot holds tile t's ocean; the other slots of that tile are not read.
All inputs are finite; a program needn't handle non-finite values. No bound on the sum of `land_mask` on one device may be relied on, other than what follows from the above.
Results may differ from a plain program's by a relative error of at most 0.0001.
Values sent between devices are 32-bit elements; how exact they have to be, the bound alone decides.
A program may use at most 64 MiB of HBM per device.

v0:
```python
import functools

import jax
import jax.numpy as jnp
import numpy as np
from jax import lax
from jax.experimental import pallas as pl
from jax.experimental.pallas import tpu as pltpu
from jax.sharding import PartitionSpec as P

NSUB = 4
DIFFUSE = 0.2
ADVECT_RATE = 0.15
CORIOLIS_MAX = 0.2
AIR_STEP = 0.05
SEA_STEP = 0.25
MESH = pl.DeviceIdType.MESH
SIGNS = (1.0, 1.0, -1.0, -1.0)


def stacked_left(mix, out_ref, pad):
    size = mix.shape[0]
    row = lax.broadcasted_iota(jnp.int32, (size, size), 0)
    col = lax.broadcasted_iota(jnp.int32, (size, size), 1)
    whole = 0.5 * mix + jnp.where(row == col, 0.5, 0.0)
    high = whole.astype(jnp.bfloat16).astype(jnp.float32)
    low = whole - high
    out_ref[...] = jnp.zeros_like(out_ref)
    out_ref[:, 0:size] = high
    out_ref[:, pad : pad + size] = high
    out_ref[:, 2 * pad : 2 * pad + size] = low


def stacked_right(cells, pad):
    size, width = cells.shape
    if pad > size:
        cells = jnp.concatenate([cells, jnp.zeros((pad - size, width), jnp.float32)], axis=0)
    high = cells.astype(jnp.bfloat16)
    low = (cells - high.astype(jnp.float32)).astype(jnp.bfloat16)
    return jnp.concatenate([high, low, high], axis=0)


def coriolis_rows(tile, tiles, rows, width):
    total = rows * tiles
    sin_tile = jnp.float32(0.0)
    cos_tile = jnp.float32(0.0)
    for index in range(tiles):
        angle = np.pi * (index * rows / total - 0.5)
        sin_tile = jnp.where(tile == index, jnp.float32(CORIOLIS_MAX * np.sin(angle)), sin_tile)
        cos_tile = jnp.where(tile == index, jnp.float32(CORIOLIS_MAX * np.cos(angle)), cos_tile)
    line = lax.broadcasted_iota(jnp.int32, (rows, width), 0)
    sin_row = jnp.zeros((rows, width), jnp.float32)
    cos_row = jnp.zeros((rows, width), jnp.float32)
    for index in range(rows):
        angle = np.pi * (index + 0.5) / total
        sin_row = jnp.where(line == index, jnp.float32(np.sin(angle)), sin_row)
        cos_row = jnp.where(line == index, jnp.float32(np.cos(angle)), cos_row)
    return sin_tile * cos_row + cos_tile * sin_row


def mix_levels(left, cells, pad):
    return jnp.dot(left, stacked_right(cells, pad), preferred_element_type=jnp.float32)


def kernel(
    members,
    tiles,
    owner_hbm,
    atm_hbm,
    ocn_hbm,
    mask_hbm,
    coef_hbm,
    air_hbm,
    sea_hbm,
    atm_out,
    ocn_out,
    state,
    halo,
    ocn,
    ocn_mixed,
    ocn_top,
    owner_ref,
    mask,
    coef,
    air,
    sea,
    cor,
    air_f32,
    sea_f32,
    air_left,
    sea_left,
    sea_share,
    top,
    push,
    surf,
    acc,
    part,
    gathered,
    spread,
    load_sem,
    halo_send,
    halo_recv,
    part_send,
    part_recv,
    spread_send,
    spread_recv,
):
    me = lax.axis_index("member")
    tile = lax.axis_index("tile")
    rows, lev, lon = state.shape[2:]
    olev = ocn.shape[2] // rows
    halves = lon // 128
    last_row = rows - 1
    air_pad = -(-lev // 16) * 16
    sea_pad = -(-olev // 16) * 16
    has_south = tile > 0
    has_north = tile < tiles - 1

    barrier = pltpu.get_barrier_semaphore()

    @pl.loop(1, members)
    def _(d):
        pl.semaphore_signal(
            barrier, inc=1, device_id=(lax.rem(me + d, members), tile), device_id_type=MESH
        )

    @pl.when(has_south)
    def _():
        pl.semaphore_signal(barrier, inc=1, device_id=(me, tile - 1), device_id_type=MESH)

    @pl.when(has_north)
    def _():
        pl.semaphore_signal(barrier, inc=1, device_id=(me, tile + 1), device_id_type=MESH)

    loads = [pltpu.make_async_copy(ocn_hbm.at[f, 0:rows], ocn_top.at[i], load_sem.at[i]) for i, f in enumerate((0, 2, 3))]
    loads += [pltpu.make_async_copy(atm_hbm.at[0, f], state.at[0, f], load_sem.at[3 + f]) for f in range(4)]
    loads += [
        pltpu.make_async_copy(mask_hbm, mask, load_sem.at[7]),
        pltpu.make_async_copy(owner_hbm, owner_ref, load_sem.at[8]),
        pltpu.make_async_copy(coef_hbm, coef, load_sem.at[9]),
        pltpu.make_async_copy(air_hbm, air, load_sem.at[10]),
        pltpu.make_async_copy(sea_hbm, sea, load_sem.at[11]),
    ]
    loads += [
        pltpu.make_async_copy(ocn_hbm.at[:, :, pl.ds(128 * h, 128)], ocn.at[:, h], load_sem.at[12 + h])
        for h in range(halves)
    ]
    for load in loads:
        load.start()

    @pl.when(jnp.logical_not(has_south))
    def _():
        @pl.loop(0, NSUB)
        def _(k):
            for f in range(4):
                halo[k, 0, f] = jnp.zeros((lev, lon), jnp.float32)

    @pl.when(jnp.logical_not(has_north))
    def _():
        @pl.loop(0, NSUB)
        def _(k):
            for f in range(4):
                halo[k, 1, f] = jnp.zeros((lev, lon), jnp.float32)

    def to_south(source, k, f):
        return pltpu.make_async_remote_copy(
            src_ref=source,
            dst_ref=halo.at[k, 1, f],
            send_sem=halo_send.at[k, 0, f],
            recv_sem=halo_recv.at[k, 1, f],
            device_id=(me, tile - 1),
            device_id_type=MESH,
        )

    def to_north(source, k, f):
        return pltpu.make_async_remote_copy(
            src_ref=source,
            dst_ref=halo.at[k, 0, f],
            send_sem=halo_send.at[k, 1, f],
            recv_sem=halo_recv.at[k, 0, f],
            device_id=(me, tile + 1),
            device_id_type=MESH,
        )

    block = part.shape[2]

    def pieces():
        for f in range(4):
            for half in range(2):
                for group in range(2):
                    index = (f * 2 + half) * 2 + group
                    place = (index * 4 // block, slice(index * 4 % block, index * 4 % block + 4))
                    yield f, slice(128 * half, 128 * half + 128), slice(4 * group, 4 * group + 4), place

    def part_copy(i, d):
        target = lax.rem(me + d, members)
        return pltpu.make_async_remote_copy(
            src_ref=part.at[i, target],
            dst_ref=gathered.at[i, d - 1],
            send_sem=part_send.at[i],
            recv_sem=part_recv.at[i],
            device_id=(target, tile),
            device_id_type=MESH,
        )

    def spread_copy(i, d):
        target = lax.rem(me + d, members)
        return pltpu.make_async_remote_copy(
            src_ref=spread.at[i, me],
            dst_ref=spread.at[i, me],
            send_sem=spread_send.at[i],
            recv_sem=spread_recv.at[i],
            device_id=(target, tile),
            device_id_type=MESH,
        )

    def all_pieces(ref, i, send, recv):
        whole = ref.at[i, pl.ds(0, members - 1)]
        return pltpu.make_async_remote_copy(
            src_ref=whole,
            dst_ref=whole,
            send_sem=send.at[i],
            recv_sem=recv.at[i],
            device_id=(lax.rem(me + 1, members), tile),
            device_id_type=MESH,
        )

    def sum_start(i, values):
        for f, cols, lines, (slot, at) in pieces():
            part[i, slot, at, :] = values[f][lines, cols]

        @pl.loop(1, members)
        def _(d):
            part_copy(i, d).start()

    def sum_middle(i):
        all_pieces(gathered, i, part_send, part_recv).wait_recv()
        total = part[i, me]
        for d in range(members - 1):
            total = total + gathered[i, d]
        spread[i, me] = total

        @pl.loop(1, members)
        def _(d):
            spread_copy(i, d).start()

    def sum_finish(i, out_ref):
        all_pieces(spread, i, spread_send, spread_recv).wait_recv()
        for f, cols, lines, (slot, at) in pieces():
            out_ref[f, lines, cols] = spread[i, slot, at, :]

    def sum_drain(i):
        all_pieces(gathered, i, part_send, part_recv).wait_send()
        all_pieces(spread, i, spread_send, spread_recv).wait_send()

    for load in loads[:3] + loads[8:9]:
        load.wait()
    owned = jnp.broadcast_to(owner_ref[...], (rows, lon)) == me
    tops = [jnp.where(owned, ocn_top[i], 0.0) for i in range(3)]
    pl.semaphore_wait(
        barrier, members - 1 + has_south.astype(jnp.int32) + has_north.astype(jnp.int32)
    )

    sum_start(0, tops + [jnp.zeros((rows, lon), jnp.float32)])
    for f in range(4):

        @pl.when(has_south)
        def _():
            to_south(atm_hbm.at[0, f, 0], 0, f).start()

        @pl.when(has_north)
        def _():
            to_north(atm_hbm.at[0, f, last_row], 0, f).start()

    for load in loads[9:12]:
        load.wait()
    cor[...] = coriolis_rows(tile, tiles, rows, lon)
    stacked_left(air[...], air_f32, air_pad)
    stacked_left(sea[...], sea_f32, sea_pad)
    air_left[...] = air_f32[...].astype(jnp.bfloat16)
    sea_left[...] = sea_f32[...].astype(jnp.bfloat16)

    for load in loads[3:8] + loads[12:]:
        load.wait()
    for f in range(4):
        top[f] = state[0, f, :, 0, :]
        acc[f] = jnp.zeros((rows, lon), jnp.float32)

    def mix_ocean(f, _):
        for r in range(rows):
            levels = pl.ds(r, olev, stride=rows)
            column = jnp.concatenate([ocn[f, h, levels, :] for h in range(halves)], axis=1)
            column = mix_levels(sea_left[...], column, sea_pad)
            for h in range(halves):
                ocn_mixed[f, h, levels, :] = column[:, 128 * h : 128 * h + 128]
        return _

    sum_middle(0)
    lax.fori_loop(0, 4, mix_ocean, 0)
    sum_finish(0, surf)
    surf[3] = coef[...] * mask[...].astype(jnp.float32)

    def fluxes():
        east = top[2] - surf[1]
        north = top[3] - surf[2]
        factor = surf[3] * jnp.sqrt(1.0 + east * east + north * north)
        values = [
            factor * (surf[0] - top[0]),
            factor * (jnp.tanh(surf[0]) - top[1]),
            factor * east,
            factor * north,
        ]
        for f in range(4):
            acc[f] = acc[f] + values[f]
            push[f] = (AIR_STEP * SIGNS[f]) * values[f]

    def advance(k, f, r, target):
        center = state[k, f, r]
        south = halo[k, 0, f] if r == 0 else state[k, f, r - 1]
        north = halo[k, 1, f] if r == last_row else state[k, f, r + 1]
        east = pltpu.roll(center, lon - 1, 1)
        west = pltpu.roll(center, 1, 1)
        spread_out = DIFFUSE * ((north + south) + (east + west)) + (1.0 - 4.0 * DIFFUSE) * center
        if f < 2:
            flow = state[k, 2, r] * (east - west) + state[k, 3, r] * (north - south)
            moved = spread_out - (0.5 * ADVECT_RATE) * flow
        else:
            turn = cor[r : r + 1, :]
            turn = turn if f == 2 else -turn
            moved = spread_out + turn * state[k, 5 - f, r]
        mixed = mix_levels(air_left[...], moved, air_pad)
        surface = mixed[0:1, :] + push[f, r : r + 1, :]
        target[f, r] = mixed
        target[f, r, 0:1, :] = surface
        top[f, r : r + 1, :] = surface

    def step(k, target, final):
        fluxes()
        if final:
            sum_start(1, [acc[f] for f in range(4)])
        for f in range(4):

            @pl.when(has_south)
            def _():
                to_north(atm_hbm.at[0, f, 0], k, f).wait_recv()

            @pl.when(has_north)
            def _():
                to_south(atm_hbm.at[0, f, 0], k, f).wait_recv()

            advance(k, f, 0, target)
            advance(k, f, last_row, target)
            if not final:

                @pl.when(has_south)
                def _():
                    to_south(target.at[f, 0], k + 1, f).start()

                @pl.when(has_north)
                def _():
                    to_north(target.at[f, last_row], k + 1, f).start()

            for r in range(1, last_row):
                advance(k, f, r, target)
            if final and f == 1:
                sum_middle(1)

    def steps(k, carry):
        step(k, state.at[k + 1], False)
        return carry

    lax.fori_loop(0, NSUB - 1, steps, 0)
    step(NSUB - 1, atm_out.at[0], True)

    sum_finish(1, acc)
    line = lax.broadcasted_iota(jnp.int32, (olev, 1), 0)
    share = SEA_STEP / (NSUB * members) * (0.5 * sea[:, 0:1] + jnp.where(line == 0, 0.5, 0.0))
    sea_share[...] = jnp.broadcast_to(share, (olev, 128))
    wet = jnp.logical_and(owned, mask[...] == 1)

    def finish_ocean(f, carry):
        forcing = acc[f]
        for level in range(olev):
            at = slice(level * rows, level * rows + rows)
            for h in range(halves):
                cols = slice(128 * h, 128 * h + 128)
                stepped = ocn_mixed[f, h, at, :] + sea_share[level : level + 1, :] * forcing[:, cols]
                ocn_out[f, at, cols] = jnp.where(wet[:, cols], stepped, ocn[f, h, at, :])
        return carry

    lax.fori_loop(0, 4, finish_ocean, 0)

    for i in range(2):
        sum_drain(i)

    @pl.loop(0, NSUB)
    def _(k):
        for f in range(4):

            @pl.when(has_south)
            def _():
                to_south(atm_hbm.at[0, f, 0], k, f).wait_send()

            @pl.when(has_north)
            def _():
                to_north(atm_hbm.at[0, f, 0], k, f).wait_send()


def shards(members, tiles, atmos_state, ocean_slots, owner_map, land_mask, transfer, air_mixing, sea_mixing):
    fields, rows, lev, lon = atmos_state.shape[1:]
    olev = ocean_slots.shape[3]
    air_pad = -(-lev // 16) * 16
    sea_pad = -(-olev // 16) * 16
    block = fields * rows * lon // 128 // members
    anywhere = pl.BlockSpec(memory_space=pltpu.MemorySpace.HBM)
    slots = ocean_slots.transpose(0, 1, 3, 2, 4).reshape(fields, olev * rows, lon)
    vmem = pl.BlockSpec(memory_space=pltpu.VMEM)
    atmos, ocean = pl.pallas_call(
        functools.partial(kernel, members, tiles),
        out_shape=(
            jax.ShapeDtypeStruct(atmos_state.shape, jnp.float32),
            jax.ShapeDtypeStruct(slots.shape, jnp.float32),
        ),
        in_specs=[anywhere] * 7,
        out_specs=(vmem, vmem),
        scratch_shapes=[
            pltpu.VMEM((NSUB, fields, rows, lev, lon), jnp.float32),
            pltpu.VMEM((NSUB, 2, fields, lev, lon), jnp.float32),
            pltpu.VMEM((fields, lon // 128, olev * rows, 128), jnp.float32),
            pltpu.VMEM((fields, lon // 128, olev * rows, 128), jnp.float32),
            pltpu.VMEM((3, rows, lon), jnp.float32),
            pltpu.VMEM((1, 1), jnp.int32),
            pltpu.VMEM((rows, lon), jnp.int32),
            pltpu.VMEM((rows, lon), jnp.float32),
            pltpu.VMEM((lev, lev), jnp.float32),
            pltpu.VMEM((olev, olev), jnp.float32),
            pltpu.VMEM((rows, lon), jnp.float32),
            pltpu.VMEM((lev, 3 * air_pad), jnp.float32),
            pltpu.VMEM((olev, 3 * sea_pad), jnp.float32),
            pltpu.VMEM((lev, 3 * air_pad), jnp.bfloat16),
            pltpu.VMEM((olev, 3 * sea_pad), jnp.bfloat16),
            pltpu.VMEM((olev, 128), jnp.float32),
            pltpu.VMEM((fields, rows, lon), jnp.float32),
            pltpu.VMEM((fields, rows, lon), jnp.float32),
            pltpu.VMEM((fields, rows, lon), jnp.float32),
            pltpu.VMEM((fields, rows, lon), jnp.float32),
            pltpu.VMEM((2, members, block, 128), jnp.float32),
            pltpu.VMEM((2, members - 1, block, 128), jnp.float32),
            pltpu.VMEM((2, members, block, 128), jnp.float32),
            pltpu.SemaphoreType.DMA((12 + lon // 128,)),
            pltpu.SemaphoreType.DMA((NSUB, 2, fields)),
            pltpu.SemaphoreType.DMA((NSUB, 2, fields)),
            pltpu.SemaphoreType.DMA((2,)),
            pltpu.SemaphoreType.DMA((2,)),
            pltpu.SemaphoreType.DMA((2,)),
            pltpu.SemaphoreType.DMA((2,)),
        ],
        compiler_params=pltpu.CompilerParams(
            collective_id=0, has_side_effects=True, vmem_limit_bytes=40 * 1024 * 1024
        ),
        name="window",
    )(
        owner_map.reshape(1, 1),
        *[
            pltpu.with_memory_space_constraint(x, pltpu.MemorySpace.HBM)
            for x in (atmos_state, slots, land_mask, transfer, air_mixing, sea_mixing)
        ],
    )
    ocean = ocean.reshape(1, fields, olev, rows, lon).transpose(0, 1, 3, 2, 4)
    return atmos, ocean


def solution(mesh):
    placed = (
        P("member", None, "tile", None, None),
        P("member", None, "tile", None, None),
        P("tile"),
        P("tile", None),
        P("tile", None),
        P(),
        P(),
    )
    return jax.shard_map(
        functools.partial(shards, mesh.shape["member"], mesh.shape["tile"]),
        mesh=mesh,
        in_specs=placed,
        out_specs=(P("member", None, "tile", None, None), P("member", None, "tile", None, None)),
        check_vma=False,
    )
```

profile of v0, /device:TPU:17, one launch (start us, length us, event | category | flops | bytes accessed | tf_op | source)
XLA Modules:
  0.0 47.2 jit_solution(7187822042057764925)
XLA Ops:
  1.3 43.2 %window.1 = (f32[1,4,8,72,256]{4,3,2,1,0:T(8,128)S(1)}, f32[4,496,256]{2,1,0:T(8,128)S(1)}) custom-call(s32[1,1]{1,0:T(1,128)} %bitcast.7.owner_hbm, f32[1,4,8,72,256]{4,3,2,1,0:T(8,128)} %atm_hbm.1, f32[4,496,256]{2,1,0:T(8,128)} %bitcast.9, s32[8,256]{1,0:T(8,128)} %mask_hbm.1, f32[8,256]{1,0:T(8,128)} %coef_hbm.1, f32[72,72]{1,0:T(8,128)} %air_hbm.1, ...), custom_call_target="tpu_custom_call" | custom-call | tf_op jit(solution)/shard_map/window/pallas_call | solution.py:418
  44.5 1.4 %copy.12 = f32[1,4,8,72,256]{4,3,2,1,0:T(8,128)} copy(f32[1,4,8,72,256]{4,3,2,1,0:T(8,128)S(1)} %get-tuple-element.8) | data formatting | bytes 4718592
  45.9 1.3 %copy.13 = f32[1,4,8,62,256]{4,2,3,1,0:T(8,128)} copy(f32[1,4,8,62,256]{4,2,3,1,0:T(8,128)S(1)} %bitcast.8) | data formatting | bytes 4063232
where the time goes:
time: 47.3 us; the launch traced here: 47.2 us
  Pallas kernels  43.2 us (91%)
  local copies, waits for them, and re-layouts  2.7 us (6%)
  between operations  1.29 us (3%)
    pallas_call x1, Pallas kernels, shards(): pl.pallas_call(functools.partial(kernel, members, tiles), out_shape=(jax....  43.2 us
    unnamed x2, local copies, waits for them, and re-layouts  2.7 us

commit v1 on v0

--- a/solution.py
+++ b/solution.py
@@ -73,11 +73,11 @@
     air_hbm,
     sea_hbm,
     atm_out,
-    ocn_out,
+    ocn,
+    sea_share,
+    forcing,
     state,
     halo,
-    ocn,
-    ocn_mixed,
     ocn_top,
     owner_ref,
     mask,
@@ -89,7 +89,6 @@
     sea_f32,
     air_left,
     sea_left,
-    sea_share,
     top,
     push,
     surf,
@@ -148,20 +147,6 @@
     for load in loads:
         load.start()
 
-    @pl.when(jnp.logical_not(has_south))
-    def _():
-        @pl.loop(0, NSUB)
-        def _(k):
-            for f in range(4):
-                halo[k, 0, f] = jnp.zeros((lev, lon), jnp.float32)
-
-    @pl.when(jnp.logical_not(has_north))
-    def _():
-        @pl.loop(0, NSUB)
-        def _(k):
-            for f in range(4):
-                halo[k, 1, f] = jnp.zeros((lev, lon), jnp.float32)
-
     def to_south(source, k, f):
         return pltpu.make_async_remote_copy(
             src_ref=source,
@@ -244,10 +229,11 @@
         def _(d):
             spread_copy(i, d).start()
 
-    def sum_finish(i, out_ref):
+    def sum_finish(i, out_ref, fields):
         all_pieces(spread, i, spread_send, spread_recv).wait_recv()
         for f, cols, lines, (slot, at) in pieces():
-            out_ref[f, lines, cols] = spread[i, slot, at, :]
+            if f < fields:
+                out_ref[f, lines, cols] = spread[i, slot, at, :]
 
     def sum_drain(i):
         all_pieces(gathered, i, part_send, part_recv).wait_send()
@@ -272,6 +258,20 @@
         def _():
             to_north(atm_hbm.at[0, f, last_row], 0, f).start()
 
+    @pl.when(jnp.logical_not(has_south))
+    def _():
+        @pl.loop(0, NSUB)
+        def _(k):
+            for f in range(4):
+                halo[k, 0, f] = jnp.zeros((lev, lon), jnp.float32)
+
+    @pl.when(jnp.logical_not(has_north))
+    def _():
+        @pl.loop(0, NSUB)
+        def _(k):
+            for f in range(4):
+                halo[k, 1, f] = jnp.zeros((lev, lon), jnp.float32)
+
     for load in loads[9:12]:
         load.wait()
     cor[...] = coriolis_rows(tile, tiles, rows, lon)
@@ -279,26 +279,6 @@
     stacked_left(sea[...], sea_f32, sea_pad)
     air_left[...] = air_f32[...].astype(jnp.bfloat16)
     sea_left[...] = sea_f32[...].astype(jnp.bfloat16)
-
-    for load in loads[3:8] + loads[12:]:
-        load.wait()
-    for f in range(4):
-        top[f] = state[0, f, :, 0, :]
-        acc[f] = jnp.zeros((rows, lon), jnp.float32)
-
-    def mix_ocean(f, _):
-        for r in range(rows):
-            levels = pl.ds(r, olev, stride=rows)
-            column = jnp.concatenate([ocn[f, h, levels, :] for h in range(halves)], axis=1)
-            column = mix_levels(sea_left[...], column, sea_pad)
-            for h in range(halves):
-                ocn_mixed[f, h, levels, :] = column[:, 128 * h : 128 * h + 128]
-        return _
-
-    sum_middle(0)
-    lax.fori_loop(0, 4, mix_ocean, 0)
-    sum_finish(0, surf)
-    surf[3] = coef[...] * mask[...].astype(jnp.float32)
 
     def fluxes():
         east = top[2] - surf[1]
@@ -314,7 +294,7 @@
             acc[f] = acc[f] + values[f]
             push[f] = (AIR_STEP * SIGNS[f]) * values[f]
 
-    def advance(k, f, r, target):
+    def advance(k, f, r, target, pushed):
         center = state[k, f, r]
         south = halo[k, 0, f] if r == 0 else state[k, f, r - 1]
         north = halo[k, 1, f] if r == last_row else state[k, f, r + 1]
@@ -329,66 +309,110 @@
             turn = turn if f == 2 else -turn
             moved = spread_out + turn * state[k, 5 - f, r]
         mixed = mix_levels(air_left[...], moved, air_pad)
-        surface = mixed[0:1, :] + push[f, r : r + 1, :]
         target[f, r] = mixed
+        if pushed:
+            push_row(f, r, target, mixed[0:1, :])
+
+    def push_row(f, r, target, line):
+        surface = line + push[f, r : r + 1, :]
         target[f, r, 0:1, :] = surface
         top[f, r : r + 1, :] = surface
 
-    def step(k, target, final):
-        fluxes()
-        if final:
-            sum_start(1, [acc[f] for f in range(4)])
-        for f in range(4):
-
-            @pl.when(has_south)
-            def _():
-                to_north(atm_hbm.at[0, f, 0], k, f).wait_recv()
-
-            @pl.when(has_north)
-            def _():
-                to_south(atm_hbm.at[0, f, 0], k, f).wait_recv()
-
-            advance(k, f, 0, target)
-            advance(k, f, last_row, target)
-            if not final:
-
-                @pl.when(has_south)
-                def _():
-                    to_south(target.at[f, 0], k + 1, f).start()
-
-                @pl.when(has_north)
-                def _():
-                    to_north(target.at[f, last_row], k + 1, f).start()
-
-            for r in range(1, last_row):
-                advance(k, f, r, target)
-            if final and f == 1:
-                sum_middle(1)
-
-    def steps(k, carry):
-        step(k, state.at[k + 1], False)
+    def interior(k, f, target, pushed):
+        for r in range(1, last_row):
+            advance(k, f, r, target, pushed)
+
+    def boundary(k, f, target, pushed):
+        @pl.when(has_south)
+        def _():
+            to_north(atm_hbm.at[0, f, 0], k, f).wait_recv()
+
+        @pl.when(has_north)
+        def _():
+            to_south(atm_hbm.at[0, f, 0], k, f).wait_recv()
+
+        advance(k, f, 0, target, pushed)
+        advance(k, f, last_row, target, pushed)
+
+    def send(k, f, target):
+        @pl.when(has_south)
+        def _():
+            to_south(target.at[f, 0], k, f).start()
+
+        @pl.when(has_north)
+        def _():
+            to_north(target.at[f, last_row], k, f).start()
+
+    for load in loads[3:7]:
+        load.wait()
+    for f in range(4):
+        top[f] = state[0, f, :, 0, :]
+        acc[f] = jnp.zeros((rows, lon), jnp.float32)
+    first = state.at[1]
+    for f in range(4):
+        interior(0, f, first, False)
+    sum_middle(0)
+
+    for load in loads[7:8] + loads[12:]:
+        load.wait()
+    wet = jnp.logical_and(owned, mask[...] == 1)
+    push[0] = jnp.where(wet, 1.0, 0.0)
+
+    def mix_ocean(f, carry):
+        for r in range(rows):
+            levels = pl.ds(r, olev, stride=rows)
+            column = jnp.concatenate([ocn[f, h, levels, :] for h in range(halves)], axis=1)
+            mixed = mix_levels(sea_left[...], column, sea_pad)
+            chosen = jnp.broadcast_to(push[0, r : r + 1, :], (olev, lon)) > 0.5
+            column = jnp.where(chosen, mixed, column)
+            for h in range(halves):
+                ocn[f, h, levels, :] = column[:, 128 * h : 128 * h + 128]
         return carry
 
-    lax.fori_loop(0, NSUB - 1, steps, 0)
-    step(NSUB - 1, atm_out.at[0], True)
-
-    sum_finish(1, acc)
+    lax.fori_loop(0, 4, mix_ocean, 0)
     line = lax.broadcasted_iota(jnp.int32, (olev, 1), 0)
     share = SEA_STEP / (NSUB * members) * (0.5 * sea[:, 0:1] + jnp.where(line == 0, 0.5, 0.0))
     sea_share[...] = jnp.broadcast_to(share, (olev, 128))
-    wet = jnp.logical_and(owned, mask[...] == 1)
-
-    def finish_ocean(f, carry):
-        forcing = acc[f]
-        for level in range(olev):
-            at = slice(level * rows, level * rows + rows)
-            for h in range(halves):
-                cols = slice(128 * h, 128 * h + 128)
-                stepped = ocn_mixed[f, h, at, :] + sea_share[level : level + 1, :] * forcing[:, cols]
-                ocn_out[f, at, cols] = jnp.where(wet[:, cols], stepped, ocn[f, h, at, :])
+
+    boundary(0, 0, first, False)
+    boundary(0, 1, first, False)
+    surf[3] = coef[...] * mask[...].astype(jnp.float32)
+    sum_finish(0, surf, 3)
+    fluxes()
+    for f in range(4):
+        if f >= 2:
+            boundary(0, f, first, False)
+        for r in (0, last_row):
+            push_row(f, r, first, first[f, r, 0:1, :])
+        send(1, f, first)
+    for f in range(4):
+        for r in range(1, last_row):
+            push_row(f, r, first, first[f, r, 0:1, :])
+
+    def middle(k, carry):
+        target = state.at[k + 1]
+        fluxes()
+        for f in range(4):
+            interior(k, f, target, True)
+            boundary(k, f, target, True)
+            send(k + 1, f, target)
         return carry
 
-    lax.fori_loop(0, 4, finish_ocean, 0)
+    lax.fori_loop(1, NSUB - 1, middle, 0)
+
+    last = atm_out.at[0]
+    fluxes()
+    sum_start(1, [acc[f] for f in range(4)])
+    for f in range(4):
+        interior(NSUB - 1, f, last, True)
+        boundary(NSUB - 1, f, last, True)
+        if f == 1:
+            sum_middle(1)
+
+    sum_finish(1, acc, 4)
+
+    for f in range(4):
+        forcing[f] = jnp.where(wet, acc[f], 0.0)
 
     for i in range(2):
         sum_drain(i)
@@ -404,6 +428,28 @@
             @pl.when(has_north)
             def _():
                 to_north(atm_hbm.at[0, f, 0], k, f).wait_send()
+
+
+def put(atmos, base, share, forcing, atmos_out, ocean_out, ocean, sem):
+    fields, halves, lines, _ = base.shape
+    rows = forcing.shape[1]
+    copies = [pltpu.make_async_copy(atmos.at[0, f], atmos_out.at[0, f], sem.at[f]) for f in range(fields)]
+    for copy in copies:
+        copy.start()
+    for f in range(fields):
+        for h in range(halves):
+            cols = slice(128 * h, 128 * h + 128)
+            flux = forcing[f, :, cols]
+            for level in range(lines // rows):
+                at = slice(level * rows, level * rows + rows)
+                ocean[f, h, at, :] = base[f, h, at, :] + share[level : level + 1, :] * flux
+            copy = pltpu.make_async_copy(
+                ocean.at[f, h], ocean_out.at[f, :, pl.ds(128 * h, 128)], sem.at[fields + f * halves + h]
+            )
+            copy.start()
+            copies.append(copy)
+    for copy in copies:
+        copy.wait()
 
 
 def shards(members, tiles, atmos_state, ocean_slots, owner_map, land_mask, transfer, air_mixing, sea_mixing):
@@ -415,19 +461,21 @@
     anywhere = pl.BlockSpec(memory_space=pltpu.MemorySpace.HBM)
     slots = ocean_slots.transpose(0, 1, 3, 2, 4).reshape(fields, olev * rows, lon)
     vmem = pl.BlockSpec(memory_space=pltpu.VMEM)
-    atmos, ocean = pl.pallas_call(
+    halves = lon // 128
+    base_shape = (fields, halves, olev * rows, 128)
+    atmos, base, share, forcing = pl.pallas_call(
         functools.partial(kernel, members, tiles),
         out_shape=(
             jax.ShapeDtypeStruct(atmos_state.shape, jnp.float32),
-            jax.ShapeDtypeStruct(slots.shape, jnp.float32),
+            jax.ShapeDtypeStruct(base_shape, jnp.float32),
+            jax.ShapeDtypeStruct((olev, 128), jnp.float32),
+            jax.ShapeDtypeStruct((fields, rows, lon), jnp.float32),
         ),
         in_specs=[anywhere] * 7,
-        out_specs=(vmem, vmem),
+        out_specs=(vmem,) * 4,
         scratch_shapes=[
             pltpu.VMEM((NSUB, fields, rows, lev, lon), jnp.float32),
             pltpu.VMEM((NSUB, 2, fields, lev, lon), jnp.float32),
-            pltpu.VMEM((fields, lon // 128, olev * rows, 128), jnp.float32),
-            pltpu.VMEM((fields, lon // 128, olev * rows, 128), jnp.float32),
             pltpu.VMEM((3, rows, lon), jnp.float32),
             pltpu.VMEM((1, 1), jnp.int32),
             pltpu.VMEM((rows, lon), jnp.int32),
@@ -439,7 +487,6 @@
             pltpu.VMEM((olev, 3 * sea_pad), jnp.float32),
             pltpu.VMEM((lev, 3 * air_pad), jnp.bfloat16),
             pltpu.VMEM((olev, 3 * sea_pad), jnp.bfloat16),
-            pltpu.VMEM((olev, 128), jnp.float32),
             pltpu.VMEM((fields, rows, lon), jnp.float32),
             pltpu.VMEM((fields, rows, lon), jnp.float32),
             pltpu.VMEM((fields, rows, lon), jnp.float32),
@@ -466,6 +513,21 @@
             for x in (atmos_state, slots, land_mask, transfer, air_mixing, sea_mixing)
         ],
     )
+    atmos, ocean = pl.pallas_call(
+        put,
+        out_shape=(
+            jax.ShapeDtypeStruct(atmos_state.shape, jnp.float32),
+            jax.ShapeDtypeStruct(slots.shape, jnp.float32),
+        ),
+        in_specs=[vmem] * 4,
+        out_specs=(anywhere, anywhere),
+        scratch_shapes=[
+            pltpu.VMEM(base_shape, jnp.float32),
+            pltpu.SemaphoreType.DMA((fields * (1 + halves),)),
+        ],
+        compiler_params=pltpu.CompilerParams(vmem_limit_bytes=8 * 1024 * 1024),
+        name="put",
+    )(atmos, base, share, forcing)
     ocean = ocean.reshape(1, fields, olev, rows, lon).transpose(0, 1, 3, 2, 4)
     return atmos, ocean
 

time: 47.3 us -> 46.1 us (0.975)
  local copies, waits for them, and re-layouts: 2.7 us -> 0 us
  Pallas kernels: 43.2 us -> 44.7 us
    unnamed x2 -> x0, local copies, waits for them, and re-layouts: 2.7 us -> none
    pallas_call x0 -> x1, Pallas kernels: none -> 2.16 us  [shards(): pl.pallas_call(put, out_shape=(jax.ShapeDtypeStruct(atmos_state.shape, jn...]
    pallas_call x1, Pallas kernels: 43.2 us -> 42.6 us  [shards(): pl.pallas_call(functools.partial(kernel, members, tiles), out_shape=(jax....]
where the time goes in v1:
time: 46.1 us; the launch traced here: 46 us
  Pallas kernels  44.7 us (97%)
  between operations  1.28 us (3%)
    pallas_call x1, Pallas kernels, shards(): pl.pallas_call(functools.partial(kernel, members, tiles), out_shape=(jax....  42.6 us
    pallas_call x1, Pallas kernels, shards(): pl.pallas_call(put, out_shape=(jax.ShapeDtypeStruct(atmos_state.shape, jn...  2.16 us

profile of v1, /device:TPU:17, one launch (start us, length us, event | category | flops | bytes accessed | tf_op | source)
XLA Modules:
  0.0 46.0 jit_solution(17910898402007485823)
XLA Ops:
  1.3 42.6 %window.1 = (f32[1,4,8,72,256]{4,3,2,1,0:T(8,128)S(1)}, f32[4,2,496,128]{3,2,1,0:T(8,128)S(1)}, f32[62,128]{1,0:T(8,128)S(1)}, f32[4,8,256]{2,1,0:T(8,128)S(1)}) custom-call(s32[1,1]{1,0:T(1,128)} %bitcast.7.owner_hbm, f32[1,4,8,72,256]{4,3,2,1,0:T(8,128)} %atm_hbm.1, f32[4,496,256]{2,1,0:T(8,128)} %bitcast.8, s32[8,256]{1,0:T(8,128)} %mask_hbm.1, ...), custom_call_target="tpu_custom_call" | custom-call | tf_op jit(solution)/shard_map/window/pallas_call | solution.py:466
  43.9 2.2 %put.1 = (f32[1,4,8,72,256]{4,3,2,1,0:T(8,128)}, f32[4,496,256]{2,1,0:T(8,128)}) custom-call(f32[1,4,8,72,256]{4,3,2,1,0:T(8,128)S(1)} %get-tuple-element.8.atmos, f32[4,2,496,128]{3,2,1,0:T(8,128)S(1)} %get-tuple-element.9.base, f32[62,128]{1,0:T(8,128)S(1)} %get-tuple-element.10.share, f32[4,8,256]{2,1,0:T(8,128)S(1)} %get-tuple-element.11.forcing), custom_call_target="tpu_custom_call" | custom-call | tf_op jit(solution)/shard_map/put/pallas_call | solution.py:516

commit v2 on v1

--- a/solution.py
+++ b/solution.py
@@ -78,6 +78,9 @@
     forcing,
     state,
     halo,
+    edge_own,
+    edge_mate,
+    edge,
     ocn_top,
     owner_ref,
     mask,
@@ -103,6 +106,10 @@
     part_recv,
     spread_send,
     spread_recv,
+    edge_send,
+    edge_recv,
+    mate_send,
+    mate_recv,
 ):
     me = lax.axis_index("member")
     tile = lax.axis_index("tile")
@@ -114,6 +121,8 @@
     sea_pad = -(-olev // 16) * 16
     has_south = tile > 0
     has_north = tile < tiles - 1
+    early = jnp.logical_and(has_south, has_north)
+    late = jnp.logical_not(early)
 
     barrier = pltpu.get_barrier_semaphore()
 
@@ -167,6 +176,41 @@
             device_id_type=MESH,
         )
 
+    half = members // 2
+    mine = lax.rem(me, half)
+    base = me - mine
+
+    def mate_copy():
+        return pltpu.make_async_remote_copy(
+            src_ref=edge_own,
+            dst_ref=edge_mate,
+            send_sem=mate_send.at[0],
+            recv_sem=mate_recv.at[0],
+            device_id=(lax.rem(me + half, members), tile),
+            device_id_type=MESH,
+        )
+
+    def edge_copy(d):
+        return pltpu.make_async_remote_copy(
+            src_ref=edge.at[mine],
+            dst_ref=edge.at[mine],
+            send_sem=edge_send.at[0],
+            recv_sem=edge_recv.at[0],
+            device_id=(base + lax.rem(mine + d, half), tile),
+            device_id_type=MESH,
+        )
+
+    def all_edges():
+        whole = edge.at[pl.ds(0, half - 1)]
+        return pltpu.make_async_remote_copy(
+            src_ref=whole,
+            dst_ref=whole,
+            send_sem=edge_send.at[0],
+            recv_sem=edge_recv.at[0],
+            device_id=(base + lax.rem(mine + 1, half), tile),
+            device_id_type=MESH,
+        )
+
     block = part.shape[2]
 
     def pieces():
@@ -214,8 +258,7 @@
         for f, cols, lines, (slot, at) in pieces():
             part[i, slot, at, :] = values[f][lines, cols]
 
-        @pl.loop(1, members)
-        def _(d):
+        for d in sorted(range(1, members), key=lambda d: (abs(d - 3 * members // 4) > 1, abs(d - members // 2))):
             part_copy(i, d).start()
 
     def sum_middle(i):
@@ -225,8 +268,7 @@
             total = total + gathered[i, d]
         spread[i, me] = total
 
-        @pl.loop(1, members)
-        def _(d):
+        for d in sorted(range(1, members), key=lambda d: (abs(d - 3 * members // 4) > 1, abs(d - members // 2))):
             spread_copy(i, d).start()
 
     def sum_finish(i, out_ref, fields):
@@ -284,15 +326,20 @@
         east = top[2] - surf[1]
         north = top[3] - surf[2]
         factor = surf[3] * jnp.sqrt(1.0 + east * east + north * north)
-        values = [
+        return [
             factor * (surf[0] - top[0]),
             factor * (jnp.tanh(surf[0]) - top[1]),
             factor * east,
             factor * north,
         ]
+
+    def set_push(values):
+        for f in range(4):
+            push[f] = (AIR_STEP * SIGNS[f]) * values[f]
+
+    def accumulate(values):
         for f in range(4):
             acc[f] = acc[f] + values[f]
-            push[f] = (AIR_STEP * SIGNS[f]) * values[f]
 
     def advance(k, f, r, target, pushed):
         center = state[k, f, r]
@@ -378,7 +425,9 @@
     boundary(0, 1, first, False)
     surf[3] = coef[...] * mask[...].astype(jnp.float32)
     sum_finish(0, surf, 3)
-    fluxes()
+    values = fluxes()
+    set_push(values)
+    accumulate(values)
     for f in range(4):
         if f >= 2:
             boundary(0, f, first, False)
@@ -389,33 +438,96 @@
         for r in range(1, last_row):
             push_row(f, r, first, first[f, r, 0:1, :])
 
-    def middle(k, carry):
-        target = state.at[k + 1]
-        fluxes()
+    target = state.at[2]
+    values = fluxes()
+    set_push(values)
+    accumulate(values)
+    for f in range(4):
+        interior(1, f, target, True)
+        boundary(1, f, target, True)
+        send(2, f, target)
+
+    target = state.at[3]
+    values = fluxes()
+    set_push(values)
+    accumulate(values)
+    line = lax.broadcasted_iota(jnp.int32, (rows, lon), 0)
+    inner = jnp.logical_and(line > 0, line < last_row)
+    interior(2, 0, target, True)
+    for f in range(4):
+        boundary(2, f, target, True)
+        send(3, f, target)
+        if f == 0:
+            interior(2, 1, target, True)
+            interior(2, 2, target, True)
+        if f == 1:
+            interior(2, 3, target, True)
+            values = fluxes()
+            ahead = [acc[g] + jnp.where(inner, values[g], 0.0) for g in range(4)]
+
+            @pl.when(early)
+            def _():
+                sum_start(1, ahead)
+
+    last = atm_out.at[0]
+    values = fluxes()
+    set_push(values)
+    whole = [acc[f] + values[f] for f in range(4)]
+
+    @pl.when(late)
+    def _():
+        sum_start(1, whole)
+
+    @pl.when(early)
+    def _():
         for f in range(4):
-            interior(k, f, target, True)
-            boundary(k, f, target, True)
-            send(k + 1, f, target)
-        return carry
-
-    lax.fori_loop(1, NSUB - 1, middle, 0)
-
-    last = atm_out.at[0]
-    fluxes()
-    sum_start(1, [acc[f] for f in range(4)])
-    for f in range(4):
-        interior(NSUB - 1, f, last, True)
-        boundary(NSUB - 1, f, last, True)
+            edge_own[2 * f : 2 * f + 1, :] = values[f][0:1, :]
+            edge_own[2 * f + 1 : 2 * f + 2, :] = values[f][last_row:rows, :]
+        mate_copy().start()
+
+    interior(3, 0, last, True)
+    boundary(3, 0, last, True)
+
+    @pl.when(early)
+    def _():
+        mate_copy().wait_recv()
+        edge[mine] = edge_own[...] + edge_mate[...]
+        for d in range(1, half):
+            edge_copy(d).start()
+        sum_middle(1)
+
+    for f in range(1, 4):
+        interior(3, f, last, True)
+        boundary(3, f, last, True)
         if f == 1:
-            sum_middle(1)
+
+            @pl.when(late)
+            def _():
+                sum_middle(1)
 
     sum_finish(1, acc, 4)
+
+    @pl.when(early)
+    def _():
+        all_edges().wait_recv()
+        total = edge[0]
+        for m in range(1, half):
+            total = total + edge[m]
+        for f in range(4):
+            acc[f, 0:1, :] = acc[f, 0:1, :] + total[2 * f : 2 * f + 1, :]
+            acc[f, last_row:rows, :] = acc[f, last_row:rows, :] + total[2 * f + 1 : 2 * f + 2, :]
 
     for f in range(4):
         forcing[f] = jnp.where(wet, acc[f], 0.0)
 
     for i in range(2):
         sum_drain(i)
+
+    @pl.when(early)
+    def _():
+        all_edges().wait_send()
+        mate_copy().wait_send()
+
 
     @pl.loop(0, NSUB)
     def _(k):
@@ -476,6 +588,9 @@
         scratch_shapes=[
             pltpu.VMEM((NSUB, fields, rows, lev, lon), jnp.float32),
             pltpu.VMEM((NSUB, 2, fields, lev, lon), jnp.float32),
+            pltpu.VMEM((2 * fields, lon), jnp.float32),
+            pltpu.VMEM((2 * fields, lon), jnp.float32),
+            pltpu.VMEM((members // 2, 2 * fields, lon), jnp.float32),
             pltpu.VMEM((3, rows, lon), jnp.float32),
             pltpu.VMEM((1, 1), jnp.int32),
             pltpu.VMEM((rows, lon), jnp.int32),
@@ -501,6 +616,10 @@
             pltpu.SemaphoreType.DMA((2,)),
             pltpu.SemaphoreType.DMA((2,)),
             pltpu.SemaphoreType.DMA((2,)),
+            pltpu.SemaphoreType.DMA((1,)),
+            pltpu.SemaphoreType.DMA((1,)),
+            pltpu.SemaphoreType.DMA((1,)),
+            pltpu.SemaphoreType.DMA((1,)),
         ],
         compiler_params=pltpu.CompilerParams(
             collective_id=0, has_side_effects=True, vmem_limit_bytes=40 * 1024 * 1024

time: 46.1 us -> 44.9 us (0.974)
  Pallas kernels: 44.7 us -> 43.5 us
    pallas_call x1, Pallas kernels: 42.6 us -> 41.3 us  [shards(): pl.pallas_call(functools.partial(kernel, members, tiles), out_shape=(jax....]
where the time goes in v2:
time: 44.9 us; the launch traced here: 44.8 us
  Pallas kernels  43.5 us (97%)
  between operations  1.28 us (3%)
    pallas_call x1, Pallas kernels, shards(): pl.pallas_call(functools.partial(kernel, members, tiles), out_shape=(jax....  41.3 us
    pallas_call x1, Pallas kernels, shards(): pl.pallas_call(put, out_shape=(jax.ShapeDtypeStruct(atmos_state.shape, jn...  2.16 us

profile of v2, /device:TPU:17, one launch (start us, length us, event | category | flops | bytes accessed | tf_op | source)
XLA Modules:
  0.0 44.8 jit_solution(10806453399781544583)
XLA Ops:
  1.3 41.3 %window.1 = (f32[1,4,8,72,256]{4,3,2,1,0:T(8,128)S(1)}, f32[4,2,496,128]{3,2,1,0:T(8,128)S(1)}, f32[62,128]{1,0:T(8,128)S(1)}, f32[4,8,256]{2,1,0:T(8,128)S(1)}) custom-call(s32[1,1]{1,0:T(1,128)} %bitcast.7.owner_hbm, f32[1,4,8,72,256]{4,3,2,1,0:T(8,128)} %atm_hbm.1, f32[4,496,256]{2,1,0:T(8,128)} %bitcast.8, s32[8,256]{1,0:T(8,128)} %mask_hbm.1, ...), custom_call_target="tpu_custom_call" | custom-call | tf_op jit(solution)/shard_map/window/pallas_call | solution.py:578
  42.6 2.2 %put.1 = (f32[1,4,8,72,256]{4,3,2,1,0:T(8,128)}, f32[4,496,256]{2,1,0:T(8,128)}) custom-call(f32[1,4,8,72,256]{4,3,2,1,0:T(8,128)S(1)} %get-tuple-element.8.atmos, f32[4,2,496,128]{3,2,1,0:T(8,128)S(1)} %get-tuple-element.9.base, f32[62,128]{1,0:T(8,128)S(1)} %get-tuple-element.10.share, f32[4,8,256]{2,1,0:T(8,128)S(1)} %get-tuple-element.11.forcing), custom_call_target="tpu_custom_call" | custom-call | tf_op jit(solution)/shard_map/put/pallas_call | solution.py:635

commit v3 on v2

--- a/solution.py
+++ b/solution.py
@@ -469,6 +469,17 @@
             def _():
                 sum_start(1, ahead)
 
+    def rows_left(k):
+        for f in range(4):
+
+            @pl.when(has_south)
+            def _():
+                to_south(atm_hbm.at[0, f, 0], k, f).wait_send()
+
+            @pl.when(has_north)
+            def _():
+                to_north(atm_hbm.at[0, f, 0], k, f).wait_send()
+
     last = atm_out.at[0]
     values = fluxes()
     set_push(values)
@@ -504,6 +515,10 @@
             @pl.when(late)
             def _():
                 sum_middle(1)
+
+            for k in range(NSUB - 1):
+                rows_left(k)
+            sum_drain(0)
 
     sum_finish(1, acc, 4)
 
@@ -520,8 +535,7 @@
     for f in range(4):
         forcing[f] = jnp.where(wet, acc[f], 0.0)
 
-    for i in range(2):
-        sum_drain(i)
+    sum_drain(1)
 
     @pl.when(early)
     def _():
@@ -529,17 +543,7 @@
         mate_copy().wait_send()
 
 
-    @pl.loop(0, NSUB)
-    def _(k):
-        for f in range(4):
-
-            @pl.when(has_south)
-            def _():
-                to_south(atm_hbm.at[0, f, 0], k, f).wait_send()
-
-            @pl.when(has_north)
-            def _():
-                to_north(atm_hbm.at[0, f, 0], k, f).wait_send()
+    rows_left(NSUB - 1)
 
 
 def put(atmos, base, share, forcing, atmos_out, ocean_out, ocean, sem):
@@ -554,12 +558,10 @@
             flux = forcing[f, :, cols]
             for level in range(lines // rows):
                 at = slice(level * rows, level * rows + rows)
-                ocean[f, h, at, :] = base[f, h, at, :] + share[level : level + 1, :] * flux
-            copy = pltpu.make_async_copy(
-                ocean.at[f, h], ocean_out.at[f, :, pl.ds(128 * h, 128)], sem.at[fields + f * halves + h]
-            )
-            copy.start()
-            copies.append(copy)
+                ocean[f, at, cols] = base[f, h, at, :] + share[level : level + 1, :] * flux
+        copy = pltpu.make_async_copy(ocean.at[f], ocean_out.at[f], sem.at[fields + f])
+        copy.start()
+        copies.append(copy)
     for copy in copies:
         copy.wait()
 
@@ -641,8 +643,8 @@
         in_specs=[vmem] * 4,
         out_specs=(anywhere, anywhere),
         scratch_shapes=[
-            pltpu.VMEM(base_shape, jnp.float32),
-            pltpu.SemaphoreType.DMA((fields * (1 + halves),)),
+            pltpu.VMEM(slots.shape, jnp.float32),
+            pltpu.SemaphoreType.DMA((2 * fields,)),
         ],
         compiler_params=pltpu.CompilerParams(vmem_limit_bytes=8 * 1024 * 1024),
         name="put",

time: 44.9 us -> 44.9 us (level)
  no operation moved by 1% of the time
where the time goes in v3:
time: 44.9 us; the launch traced here: 44.7 us
  Pallas kernels  43.4 us (97%)
  between operations  1.28 us (3%)
    pallas_call x1, Pallas kernels, shards(): pl.pallas_call(functools.partial(kernel, members, tiles), out_shape=(jax....  41.3 us
    pallas_call x1, Pallas kernels, shards(): pl.pallas_call(put, out_shape=(jax.ShapeDtypeStruct(atmos_state.shape, jn...  2.13 us

profile of v3, /device:TPU:17, one launch (start us, length us, event | category | flops | bytes accessed | tf_op | source)
XLA Modules:
  0.0 44.7 jit_solution(2683253738127173907)
XLA Ops:
  1.3 41.3 %window.1 = (f32[1,4,8,72,256]{4,3,2,1,0:T(8,128)S(1)}, f32[4,2,496,128]{3,2,1,0:T(8,128)S(1)}, f32[62,128]{1,0:T(8,128)S(1)}, f32[4,8,256]{2,1,0:T(8,128)S(1)}) custom-call(s32[1,1]{1,0:T(1,128)} %bitcast.7.owner_hbm, f32[1,4,8,72,256]{4,3,2,1,0:T(8,128)} %atm_hbm.1, f32[4,496,256]{2,1,0:T(8,128)} %bitcast.8, s32[8,256]{1,0:T(8,128)} %mask_hbm.1, ...), custom_call_target="tpu_custom_call" | custom-call | tf_op jit(solution)/shard_map/window/pallas_call | solution.py:580
  42.6 2.1 %put.1 = (f32[1,4,8,72,256]{4,3,2,1,0:T(8,128)}, f32[4,496,256]{2,1,0:T(8,128)}) custom-call(f32[1,4,8,72,256]{4,3,2,1,0:T(8,128)S(1)} %get-tuple-element.8.atmos, f32[4,2,496,128]{3,2,1,0:T(8,128)S(1)} %get-tuple-element.9.base, f32[62,128]{1,0:T(8,128)S(1)} %get-tuple-element.10.share, f32[4,8,256]{2,1,0:T(8,128)S(1)} %get-tuple-element.11.forcing), custom_call_target="tpu_custom_call" | custom-call | tf_op jit(solution)/shard_map/put/pallas_call | solution.py:637
